TPU v7x, 32 devices: a whole 2x2x4 slice. The times are simulated.
32 devices in a mesh: series: 4 (over z), head: 8 (over y, x, core).
Axes of the slice: x: 2, y: 2, z: 4, core: 2. Of those that a mesh axis runs over, the one named last changes fastest.
Arguments:
- teacher_in: bfloat16 [32, 128, 4096], P(('series', 'head')), may hold values from -6 to 6
- teacher_gain: float32 [4096], replicated, may hold values from 0.5 to 1.5
- w_gate: bfloat16 [4096, 8192], P(None, 'head'), may hold values from -0.09375 to 0.09375
- w_up: bfloat16 [4096, 8192], P(None, 'head'), may hold values from -0.09375 to 0.09375
- readout: bfloat16 [8192, 1024], P('head'), may hold values from -0.0625 to 0.0625
- distill_proj: bfloat16 [4096, 1024], P('head'), may hold values from -0.09375 to 0.09375
- building_ids: int32 [32], P(('series', 'head')), may hold values from 0 to 1023
- student_in: bfloat16 [32, 128, 1024], P(('series', 'head')), may hold values from -6 to 6
- embed_rows: bfloat16 [1024, 1024], replicated, may hold values from -4 to 4
- covariates: bfloat16 [1024, 128], replicated, may hold values from -5 to 5
- cov_proj: bfloat16 [128, 1024], replicated, may hold values from -0.5 to 0.5
- student_gain: float32 [1024], replicated, may hold values from 0.25 to 1.75
- w_x: bfloat16 [1024, 2048], replicated, may hold values from -0.1875 to 0.1875
- w_bcdt: bfloat16 [1024, 288], replicated, may hold values from -0.1875 to 0.1875
- conv_w: float32 [4, 2304], replicated, may hold values from -3 to 3
- dt_bias: float32 [32], replicated, may hold values from -1 to 1
- a_log: float32 [32], replicated, may hold values from -6 to -2.5
- d_skip: float32 [32], replicated, may hold values from 0.5 to 1.5
- norm_gain: float32 [2048], replicated, may hold values from 0.25 to 1.75
- w_out: bfloat16 [2048, 1024], replicated, may hold values from -0.125 to 0.125
Outputs:
- grad_bcdt: float32 [1024, 288], P(('series', 'head'))
- grad_conv: float32 [4, 2304], P(None, ('series', 'head'))
- grad_gain: float32 [2048], P(('series', 'head'))
- grad_out: float32 [2048, 1024], P(('series', 'head'))
Inputs may be any that keep to these rules, and one draw needn't show every extreme that they name: `building_ids`: building ids index rows of the building tables.
All inputs are finite; a program needn't handle non-finite values.
Results may differ from a plain program's by a relative error of at most 0.013.
The roundings to bfloat16 on the way count: a program that leaves them out, or rounds other values in their place, can miss the bound.
Values may be sent and summed in bfloat16 or wider, within the bound.
No kernel may reach another device: no remote copies, remote signals or barrier semaphores. Data moves between devices by JAX's collectives and lax.ppermute only.
A program may use at most 128 MiB of HBM per device.

v0:
```python
from functools import partial
import jax
import jax.numpy as jnp
from jax import lax
from jax.sharding import PartitionSpec as P

EPS = 1e-05


def rms_scale(values, gain):
    mean_sq = jnp.mean(values * values, axis=-1, keepdims=True)
    return values * lax.rsqrt(mean_sq + EPS) * gain


def teacher_rows(row_block, teacher_gain, w_gate, w_up, readout, proj_rows, feat_start):
    normed = rms_scale(row_block.astype(jnp.float32), teacher_gain).astype(jnp.bfloat16)
    gate_vals = jnp.dot(normed, w_gate, preferred_element_type=jnp.float32)
    upward = jnp.dot(normed, w_up, preferred_element_type=jnp.float32)
    hidden = (jax.nn.silu(gate_vals) * upward).astype(jnp.bfloat16)
    features = lax.dynamic_slice_in_dim(row_block, feat_start, proj_rows.shape[0], 1)
    return jnp.dot(hidden, readout, preferred_element_type=jnp.float32) + jnp.dot(
        features, proj_rows, preferred_element_type=jnp.float32
    )


def mixer_core(projected, conv_w, norm_gain, x_stream, dt_bias, a_log, d_skip):
    seq_len = x_stream.shape[0]
    inner_width = x_stream.shape[1]
    head_count = dt_bias.shape[0]
    state_size = (projected.shape[1] - head_count) // 2
    head_size = inner_width // head_count
    mixture = jnp.concatenate([x_stream, projected[:, : 2 * state_size]], axis=1)
    taps = conv_w.shape[0]
    padded = jnp.pad(mixture, ((taps - 1, 0), (0, 0)))
    convolved = padded[0:seq_len] * conv_w[0]
    for offset in range(1, taps):
        convolved = convolved + padded[offset : offset + seq_len] * conv_w[offset]
    activated = jax.nn.silu(convolved)
    x_heads = activated[:, :inner_width].reshape(seq_len, head_count, head_size)
    b_state = activated[:, inner_width : inner_width + state_size]
    c_state = activated[:, inner_width + state_size :]
    dt_step = jax.nn.softplus(projected[:, 2 * state_size :] + dt_bias)
    running = jnp.cumsum(dt_step * -jnp.exp(a_log), axis=0)
    later_pos = lax.broadcasted_iota(jnp.int32, (seq_len, seq_len), 0)
    earlier_pos = lax.broadcasted_iota(jnp.int32, (seq_len, seq_len), 1)
    differences = running[:, None, :] - running[None, :, :]
    decays = jnp.exp(jnp.where((later_pos >= earlier_pos)[:, :, None], differences, -1e30))
    scores = jnp.dot(c_state, b_state.T, precision=lax.Precision.HIGHEST)
    weights = scores[:, :, None] * decays * dt_step[None, :, :]
    mixed = (
        jnp.einsum("tsh,shp->thp", weights, x_heads, precision=lax.Precision.HIGHEST)
        + d_skip[None, :, None] * x_heads
    )
    return rms_scale(mixed.reshape(seq_len, inner_width), norm_gain)


def student_terms(
    series_x,
    extra_row,
    target_rows,
    student_gain,
    w_x,
    w_bcdt,
    conv_w,
    dt_bias,
    a_log,
    d_skip,
    norm_gain,
    w_out,
    series_total,
):
    base = series_x.astype(jnp.float32) + extra_row[None, :]
    normed = rms_scale(base, student_gain).astype(jnp.bfloat16)
    x_stream = jnp.dot(normed, w_x, preferred_element_type=jnp.float32)
    projected = jnp.dot(normed, w_bcdt, preferred_element_type=jnp.float32)

    def forward(proj_in, conv_in, gain_in):
        return mixer_core(proj_in, conv_in, gain_in, x_stream, dt_bias, a_log, d_skip)

    out_norm, pullback = jax.vjp(forward, projected, conv_w, norm_gain)
    rounded = out_norm.astype(jnp.bfloat16)
    output = jnp.dot(rounded, w_out, preferred_element_type=jnp.float32)
    d_output = ((output - target_rows) / series_total).astype(jnp.bfloat16)
    d_norm = jnp.dot(d_output, w_out.T, preferred_element_type=jnp.float32)
    d_proj, g_conv, g_gain = pullback(d_norm)
    g_out = jnp.dot(rounded.T, d_output, preferred_element_type=jnp.float32)
    g_bcdt = jnp.dot(normed.T, d_proj.astype(jnp.bfloat16), preferred_element_type=jnp.float32)
    return (g_bcdt, g_conv, g_gain, g_out)


def per_device(
    teacher_in,
    teacher_gain,
    w_gate,
    w_up,
    readout,
    distill_proj,
    building_ids,
    student_in,
    embed_rows,
    covariates,
    cov_proj,
    student_gain,
    w_x,
    w_bcdt,
    conv_w,
    dt_bias,
    a_log,
    d_skip,
    norm_gain,
    w_out,
):
    own_series = teacher_in.shape[0]
    seq_len = teacher_in.shape[1]
    model_width = teacher_in.shape[2]
    series_total = own_series * lax.axis_size("series") * lax.axis_size("head")
    feat_start = lax.axis_index("head") * distill_proj.shape[0]
    row_block = lax.all_gather(teacher_in, "head", axis=0, tiled=True)
    count = row_block.shape[0]
    flat_rows = row_block.reshape(count * seq_len, model_width)
    terms = teacher_rows(flat_rows, teacher_gain, w_gate, w_up, readout, distill_proj, feat_start)
    group_terms = terms.reshape(count, seq_len, terms.shape[1])
    summed = lax.psum(group_terms, "head")
    target = lax.dynamic_slice_in_dim(summed, lax.axis_index("head") * own_series, own_series, 0)
    selector = (
        building_ids[:, None]
        == lax.broadcasted_iota(jnp.int32, (own_series, embed_rows.shape[0]), 1)
    ).astype(jnp.bfloat16)
    embedded = jnp.dot(selector, embed_rows, preferred_element_type=jnp.float32)
    cov_rows = jnp.dot(selector, covariates, preferred_element_type=jnp.float32).astype(
        jnp.bfloat16
    )
    extra = embedded + jnp.dot(cov_rows, cov_proj, preferred_element_type=jnp.float32)
    local_terms = partial(
        student_terms,
        student_gain=student_gain,
        w_x=w_x,
        w_bcdt=w_bcdt,
        conv_w=conv_w,
        dt_bias=dt_bias,
        a_log=a_log,
        d_skip=d_skip,
        norm_gain=norm_gain,
        w_out=w_out,
        series_total=series_total,
    )
    per_series = jax.vmap(local_terms)(student_in, extra, target)
    g_bcdt = jnp.sum(per_series[0], axis=0)
    g_conv = jnp.sum(per_series[1], axis=0)
    g_gain = jnp.sum(per_series[2], axis=0)
    g_out = jnp.sum(per_series[3], axis=0)
    g_bcdt, g_conv, g_gain, g_out = (
        lax.psum_scatter(g_bcdt, ("series", "head"), scatter_dimension=0, tiled=True),
        lax.psum_scatter(g_conv, ("series", "head"), scatter_dimension=1, tiled=True),
        lax.psum_scatter(g_gain, ("series", "head"), scatter_dimension=0, tiled=True),
        lax.psum_scatter(g_out, ("series", "head"), scatter_dimension=0, tiled=True),
    )
    return (g_bcdt, g_conv, g_gain, g_out)


def solution(mesh):
    return jax.shard_map(
        per_device,
        mesh=mesh,
        in_specs=(
            P(("series", "head"), None, None),
            P(),
            P(None, "head"),
            P(None, "head"),
            P("head", None),
            P("head", None),
            P(("series", "head")),
            P(("series", "head"), None, None),
            P(),
            P(),
            P(),
            P(),
            P(),
            P(),
            P(),
            P(),
            P(),
            P(),
            P(),
            P(),
        ),
        out_specs=(
            P(("series", "head"), None),
            P(None, ("series", "head")),
            P(("series", "head")),
            P(("series", "head"), None),
        ),
        check_vma=False,
    )
```

profile of v0, /device:TPU:0, one launch (start us, length us, event | category | flops | bytes accessed | tf_op | source)
XLA Modules:
  0.0 478.3 jit_solution(16399168680379305801)
XLA Ops:
  10.0 2.0 fusion.57
  13.8 3.0 convolution_bitcast_fusion
  16.8 50.2 %all-gather.2.cloned.1.call-done = bf16[8,128,4096]{2,1,0:T(8,128)(2,1)} async-done(((bf16[1,128,4096]{2,1,0:T(8,128)(2,1)}), bf16[8,128,4096]{2,1,0:T(8,128)(2,1)}) %all-gather.2.cloned.1.call-update) | async-done | bytes 8388624 | tf_op jit(solution)/shard_map/all_gather | solution.py:118
  67.1 5.2 %multiply_reduce_fusion = f32[8,128]{1,0:T(8,128)S(1)} fusion(bf16[8,128,4096]{2,1,0:T(8,128)(2,1)} %all-gather.2.cloned.1.call-done), kind=kLoop, calls=%fused_computation.1 | loop fusion | flops 12581888 | bytes 8392704 | tf_op jit(solution)/shard_map/reduce_sum | solution.py:11
  72.8 12.7 %fusion = f32[1024,1024]{1,0:T(8,128)} fusion(bf16[4096,1024]{1,0:T(8,128)(2,1)} %param.23, bf16[1024,4096]{1,0:T(8,128)(2,1)S(1)} %bitcast.132, f32[4096]{0:T(1024)} %param.21, f32[1024]{0:T(1024)S(1)} %rsqrt_bitcast_fusion), kind=kOutput, calls=%fused_computation.4 | convolution fusion | flops 8606711808 | bytes 20992000 | tf_op jit(solution)/shard_map/dot_general | solution.py:18
  85.5 18.4 %fusion.2 = f32[1024,1024]{1,0:T(8,128)} fusion(bf16[1024,1024]{1,0:T(8,128)(2,1)S(1)} %copy-done, f32[1024,1024]{1,0:T(8,128)} %fusion, bf16[4096,1024]{1,0:T(8,128)(2,1)} %param.22, bf16[1024,4096]{1,0:T(8,128)(2,1)} %bitcast.130, f32[4096]{0:T(1024)} %param.21, f32[1024]{0:T(1024)S(1)} %rsqrt_bitcast_fusion), kind=kOutput, calls=%fused_computation.6 | convolution fusion | flops 10760486912 | bytes 27283456 | tf_op jit(solution)/shard_map/dot_general | solution.py:21
  103.9 6.1 %convolution_add_fusion = f32[1024,1024]{1,0:T(8,128)} fusion(f32[1024,1024]{1,0:T(8,128)} %fusion.2, bf16[512,1024]{1,0:T(8,128)(2,1)} %param.25, bf16[1024,4096]{1,0:T(8,128)(2,1)} %bitcast.131, s32[]{:T(128)S(6)} %select_n.46), kind=kOutput, calls=%fused_computation.7 | convolution fusion | flops 1074790400 | bytes 10485764 | tf_op jit(solution)/shard_map/dot_general | solution.py:21
  111.3 1.7 fusion.18
  114.2 2.6 copy.56
  117.2 6.5 %multiply_reduce_fusion.8 = (f32[128]{0:T(128)S(1)}, f32[1,128,32,64]{1,3,2,0:T(8,128)}) fusion(f32[1,128,32,64]{1,3,2,0:T(8,128)} %bitcast.135, f32[32]{0:T(128)S(1)} %copy-done.32, f32[128,32,64]{0,2,1:T(8,128)} %bitcast.136, f32[128,32]{0,1:T(8,128)S(1)} %copy.59, f32[128,32]{0,1:T(8,128)S(1)} %copy.54, f32[128,128]{1,0:T(8,128)S(1)} %fusion.45, ...), kind=kOutput, calls=%fused_computation.55 | convolution fusion | flops 405798784 | bytes 3261056 | tf_op jit(solution)/shard_map/vmap(jvp(tsh,shp->thp))/dot_general | solution.py:51
  123.7 1.6 copy.61
  125.3 65.9 %all-reduce.19.cloned.1.call-done = f32[8,128,1024]{2,1,0:T(8,128)} async-done(((f32[8,128,1024]{2,1,0:T(8,128)}), f32[8,128,1024]{2,1,0:T(8,128)}) %all-reduce.19.cloned.1.call-update) | async-done | bytes 4194320 | tf_op jit(solution)/shard_map/psum | solution.py:123
  191.1 3.2 fusion.19
  194.7 2.2 multiply_reduce_fusion.6
  198.3 2.6 copy.64
  200.9 6.2 %fusion.12 = (f32[128,32]{0,1:T(8,128)S(1)}, f32[128,32]{0,1:T(8,128)S(1)}, f32[128,32]{0,1:T(8,128)S(1)}, f32[128,128]{1,0:T(8,128)S(1)}) fusion(f32[128,32]{0,1:T(8,128)S(1)} %copy.59, f32[128,32]{0,1:T(8,128)S(1)} %copy.54, f32[128,128]{1,0:T(8,128)S(1)} %fusion.45, pred[128,128]{1,0:T(8,128)(4,1)S(1)} %iota_compare_fusion, ...), kind=kOutput, calls=%fused_computation.26 | convolution fusion | flops 409440256 | bytes 2326528 | tf_op jit(solution)/shard_map/vmap(transpose(jvp(tsh,shp->thp)))/dot_general | solution.py:51
  209.5 4.1 fusion.9
  213.7 2.7 copy.68
  217.6 3.2 multiply_reduce_fusion.4
  222.3 1.7 fusion.40
  224.5 4.5 fusion.58
  229.8 39.9 %all-reduce.16 = (f32[4,2304]{1,0:T(4,128)S(1)}, f32[2048]{0:T(1024)S(1)}) all-reduce(f32[4,2304]{1,0:T(4,128)S(1)} %add_bitcast_fusion, f32[2048]{0:T(1024)S(1)} %copy-done.18), channel_id=3, replica_groups=mesh['series'=4,'head'=8] {'series','head'}, use_global_device_ids=true, to_apply=%region_16.17.clone | all-reduce | flops 11264 | bytes 90112
  270.9 50.3 %reduce-scatter.4.cloned.1.call-done = f32[32,288]{1,0:T(8,128)} async-done(((f32[1024,288]{1,0:T(8,128)}), f32[32,288]{1,0:T(8,128)}) %reduce-scatter.4.cloned.1.call-update) | async-done | bytes 36880 | tf_op jit(solution)/shard_map/reduce_scatter | solution.py:153
  321.2 150.5 %reduce-scatter.6.cloned.1.call-done = f32[64,1024]{1,0:T(8,128)} async-done(((f32[2048,1024]{1,0:T(8,128)}), f32[64,1024]{1,0:T(8,128)}) %reduce-scatter.6.cloned.1.call-update) | async-done | bytes 262160 | tf_op jit(solution)/shard_map/reduce_scatter | solution.py:156
  (114 shorter events, 16.6 us)
Async XLA Ops:
  7.2 78.4 %copy-start = (bf16[1024,1024]{1,0:T(8,128)(2,1)S(1)}, bf16[1024,1024]{1,0:T(8,128)(2,1)}, u32[]{:S(2)}) copy-start(bf16[1024,1024]{1,0:T(8,128)(2,1)} %param.24) | copy-start | bytes 6291460
  7.2 4.8 %copy-start.8 = (bf16[1,128,1024]{2,1,0:T(8,128)(2,1)S(1)}, bf16[1,128,1024]{2,1,0:T(8,128)(2,1)}, u32[]{:S(2)}) copy-start(bf16[1,128,1024]{2,1,0:T(8,128)(2,1)} %param.27) | copy-start | bytes 786436
  7.2 5.0 %copy-start.20 = (f32[1024]{0:T(1024)S(1)}, f32[1024]{0:T(1024)}, u32[]{:S(2)}) copy-start(f32[1024]{0:T(1024)} %param.31) | copy-start | bytes 12292
  7.2 5.0 %copy-start.30 = (bf16[1024,288]{0,1:T(8,128)(2,1)S(1)}, bf16[1024,288]{0,1:T(8,128)(2,1)}, u32[]{:S(2)}) copy-start(bf16[1024,288]{0,1:T(8,128)(2,1)} %param.33) | copy-start | bytes 1769476
  7.2 59.8 %all-gather.2.cloned.1.call-start = ((), (), s32[]{:S(2)}) async-start(), calls=%async_computation.2 | async-start | bytes 9437184 | tf_op jit(solution)/shard_map/all_gather | solution.py:118
  7.9 4.6 copy-start.31
  8.0 5.8 %copy-start.24 = (f32[32]{0:T(128)S(1)}, f32[32]{0:T(128)}, u32[]{:S(2)}) copy-start(f32[32]{0:T(128)} %param.35) | copy-start | bytes 388
  8.0 183.2 %all-reduce.19.cloned.1.call-start = ((), (), s32[]{:S(2)}) async-start(), calls=%async_computation.3 | async-start | bytes 8388608 | tf_op jit(solution)/shard_map/psum | solution.py:123
  16.8 94.4 %copy-start.4 = (f32[1,128,2048]{2,1,0:T(8,128)}, f32[1,128,2048]{2,1,0:T(8,128)S(1)}, u32[]{:S(2)}) copy-start(f32[1,128,2048]{2,1,0:T(8,128)S(1)} %convolution_bitcast_fusion) | copy-start | bytes 3145732
  67.1 5.8 %copy-start.3 = (bf16[8,128,4096]{2,1,0:T(8,128)(2,1)S(1)}, bf16[8,128,4096]{2,1,0:T(8,128)(2,1)}, u32[]{:S(2)}) copy-start(bf16[8,128,4096]{2,1,0:T(8,128)(2,1)} %all-gather.2.cloned.1.call-done) | copy-start | bytes 25165828
  110.0 211.3 %reduce-scatter.4.cloned.1.call-start = ((), (), s32[]{:S(2)}) async-start(), calls=%async_computation.4 | async-start | bytes 1622016 | tf_op jit(solution)/shard_map/reduce_scatter | solution.py:153
  113.0 3.9 copy-start.6
  113.0 4.2 copy-start.32
  116.9 84.0 %copy-start.19 = (pred[128,128]{1,0:T(8,128)(4,1)}, pred[128,128]{1,0:T(8,128)(4,1)S(1)}, u32[]{:S(2)}) copy-start(pred[128,128]{1,0:T(8,128)(4,1)S(1)} %iota_compare_fusion) | copy-start | bytes 49156
  123.7 67.5 %copy-start.13 = (f32[2048]{0:T(1024)S(1)}, f32[2048]{0:T(1024)}, u32[]{:S(2)}) copy-start(f32[2048]{0:T(1024)} %param.38) | copy-start | bytes 24580
  125.3 71.7 %copy-start.22 = (f32[128]{0:T(128)}, f32[128]{0:T(128)S(1)}, u32[]{:S(2)}) copy-start(f32[128]{0:T(128)S(1)} %fusion.47) | copy-start | bytes 1540
  191.1 3.6 copy-start.2
  198.3 2.6 copy-start.9
  200.9 8.6 %copy-start.10 = (f32[128,2048]{0,1:T(8,128)S(1)}, f32[128,2048]{0,1:T(8,128)}, u32[]{:S(2)}) copy-start(f32[128,2048]{0,1:T(8,128)} %copy.64) | copy-start | bytes 3145732
  213.7 4.0 copy-start.5
  222.3 1.8 copy-start.7
  222.3 1.8 copy-start.23
  224.0 247.8 %reduce-scatter.6.cloned.1.call-start = ((), (), s32[]{:S(2)}) async-start(), calls=%async_computation.5 | async-start | bytes 8650752 | tf_op jit(solution)/shard_map/reduce_scatter | solution.py:156
  229.0 242.8 %copy-start.1 = (bf16[1024,1024]{1,0:T(8,128)(2,1)S(1)}, bf16[1024,1024]{1,0:T(8,128)(2,1)}, u32[]{:S(2)}) copy-start(bf16[1024,1024]{1,0:T(8,128)(2,1)} %param.24) | copy-start | bytes 6291460
  (13 other events, 10.3 us)
Sparse Core Ops, SparseCore 0:
  9.9 57.0 all-gather.1
  110.1 80.9 all-reduce.18
  224.1 97.0 reduce-scatter.3
  324.1 147.6 reduce-scatter.5
where the time goes:
time: 479 us; the launch traced here: 478 us
  waiting for transfers between devices  318 us (66%)
  matrix products  74.8 us (16%)
  blocking collectives  39.9 us (8%)
  local copies, waits for them, and re-layouts  16.8 us (4%)
  between operations  14.8 us (3%)
  other arithmetic  13.9 us (3%)
    reduce_scatter x1, waiting for transfers between devices, per_device(): lax.psum_scatter(g_out, ('series', 'head'), scatter_dimension=0, tiled=True)  151 us
    psum x1, waiting for transfers between devices, per_device(): summed = lax.psum(group_terms, 'head')  65.9 us
    reduce_scatter x1, waiting for transfers between devices, per_device(): lax.psum_scatter(g_bcdt, ('series', 'head'), scatter_dimension=0, tiled=T...  50.3 us
    all_gather x1, waiting for transfers between devices, per_device(): row_block = lax.all_gather(teacher_in, 'head', axis=0, tiled=True)  50.2 us
    unnamed x1, blocking collectives  39.9 us
    dot_general x1, matrix products, teacher_rows(): jnp.dot(hidden, readout, preferred_element_type=jnp.float32)  18.4 us
    dot_general x3, matrix products, mixer_core(): jnp.einsum('tsh,shp->thp', weights, x_heads, precision=lax.Precision.HIGH...  16.8 us
    dot_general x1, matrix products, teacher_rows(): upward = jnp.dot(normed, w_up, preferred_element_type=jnp.float32)  12.7 us
  transfers between devices with their start and end apart: 4, of which 4 were waited for; matrix products, arithmetic and copies ran while one was open for 6% of the time, Pallas kernels for 0%

commit v1 on v0

--- a/solution.py
+++ b/solution.py
@@ -120,7 +120,11 @@
     flat_rows = row_block.reshape(count * seq_len, model_width)
     terms = teacher_rows(flat_rows, teacher_gain, w_gate, w_up, readout, distill_proj, feat_start)
     group_terms = terms.reshape(count, seq_len, terms.shape[1])
-    summed = lax.psum(group_terms, "head")
+    size = lax.axis_size("head")
+    summed, far = (group_terms, 1)
+    while far < size:
+        summed = summed + lax.ppermute(summed, "head", [(i, i ^ far) for i in range(size)])
+        far = 2 * far
     target = lax.dynamic_slice_in_dim(summed, lax.axis_index("head") * own_series, own_series, 0)
     selector = (
         building_ids[:, None]

time: 479 us -> 588 us (1.23)
  waiting for transfers between devices: 318 us -> 428 us
    ppermute x0 -> x3, waiting for transfers between devices: none -> 167 us  [per_device(): lax.ppermute(summed, 'head', [(i, i ^ far) for i in range(size)])]
    psum x1 -> x0, waiting for transfers between devices: 65.9 us -> none  [per_device(): summed = lax.psum(group_terms, 'head')]
    all_gather x1, waiting for transfers between devices: 50.2 us -> 59.1 us  [per_device(): row_block = lax.all_gather(teacher_in, 'head', axis=0, tiled=True)]
  transfers between devices with their start and end apart: 4 -> 6, of which waited for: 4 -> 6; matrix products, arithmetic and copies ran while one was open for 6% -> 5% of each run, Pallas kernels for 0% -> 0%
where the time goes in v1:
time: 588 us
  waiting for transfers between devices  428 us (73%)
  matrix products  70 us (12%)
  blocking collectives  39.8 us (7%)
  other arithmetic  17.6 us (3%)
  between operations  14.8 us (3%)
  local copies, waits for them, and re-layouts  14 us (2%)
    ppermute x3, waiting for transfers between devices, per_device(): lax.ppermute(summed, 'head', [(i, i ^ far) for i in range(size)])  167 us
    reduce_scatter x1, waiting for transfers between devices, per_device(): lax.psum_scatter(g_out, ('series', 'head'), scatter_dimension=0, tiled=True)  151 us
    all_gather x1, waiting for transfers between devices, per_device(): row_block = lax.all_gather(teacher_in, 'head', axis=0, tiled=True)  59.1 us
    reduce_scatter x1, waiting for transfers between devices, per_device(): lax.psum_scatter(g_bcdt, ('series', 'head'), scatter_dimension=0, tiled=T...  50.7 us
    unnamed x1, blocking collectives  39.8 us
    dot_general x1, matrix products, teacher_rows(): jnp.dot(hidden, readout, preferred_element_type=jnp.float32)  18.4 us
    dot_general x3, matrix products, mixer_core(): jnp.einsum('tsh,shp->thp', weights, x_heads, precision=lax.Precision.HIGH...  16 us
    dot_general x1, matrix products, teacher_rows(): upward = jnp.dot(normed, w_up, preferred_element_type=jnp.float32)  12.7 us
  transfers between devices with their start and end apart: 6, of which 6 were waited for; matrix products, arithmetic and copies ran while one was open for 5% of the time, Pallas kernels for 0%

profile of v1, /device:TPU:0, one launch (start us, length us, event | category | flops | bytes accessed | tf_op | source)
XLA Modules:
  0.0 587.9 jit_solution(12139573792179437848)
XLA Ops:
  8.0 59.1 %all-gather.2.cloned.1.call-done = bf16[8,128,4096]{2,1,0:T(8,128)(2,1)} async-done(((bf16[1,128,4096]{2,1,0:T(8,128)(2,1)}), bf16[8,128,4096]{2,1,0:T(8,128)(2,1)}) %all-gather.2.cloned.1.call-update) | async-done | bytes 8388624 | tf_op jit(solution)/shard_map/all_gather | solution.py:118
  67.0 5.2 multiply_reduce_fusion
  72.8 12.7 %fusion = f32[1024,1024]{1,0:T(8,128)} fusion(bf16[4096,1024]{1,0:T(8,128)(2,1)} %param.23, bf16[1024,4096]{1,0:T(8,128)(2,1)S(1)} %bitcast.129, f32[4096]{0:T(1024)S(1)} %copy-done.19, f32[1024]{0:T(1024)S(1)} %rsqrt_bitcast_fusion), kind=kOutput, calls=%fused_computation.4 | convolution fusion | flops 8606711808 | bytes 20992000 | tf_op jit(solution)/shard_map/dot_general | solution.py:18
  85.5 18.4 %fusion.2 = f32[1024,1024]{1,0:T(8,128)} fusion(bf16[1024,1024]{1,0:T(8,128)(2,1)S(1)} %copy-done, f32[1024,1024]{1,0:T(8,128)} %fusion, bf16[4096,1024]{1,0:T(8,128)(2,1)} %param.22, bf16[1024,4096]{1,0:T(8,128)(2,1)} %bitcast.127, f32[4096]{0:T(1024)S(1)} %copy-done.19, f32[1024]{0:T(1024)S(1)} %rsqrt_bitcast_fusion), kind=kOutput, calls=%fused_computation.6 | convolution fusion | flops 10760486912 | bytes 27283456 | tf_op jit(solution)/shard_map/dot_general | solution.py:21
  103.8 3.8 convolution_add_fusion
  107.9 6.9 %collective-permute-done = f32[8,128,1024]{2,1,0:T(8,128)S(1)} collective-permute-done((f32[8,128,1024]{2,1,0:T(8,128)S(1)}, f32[8,128,1024]{2,1,0:T(8,128)S(1)}, u32[]{:S(2)}, u32[]{:S(2)}) %collective-permute-start) | collective-permute-done | bytes 4194336 | tf_op jit(solution)/shard_map/ppermute | solution.py:126
  117.8 91.3 %collective-permute-done.1 = f32[8,128,1024]{2,1,0:T(8,128)S(1)} collective-permute-done((f32[8,128,1024]{2,1,0:T(8,128)S(1)}, f32[8,128,1024]{2,1,0:T(8,128)S(1)}, u32[]{:S(2)}, u32[]{:S(2)}) %collective-permute-start.1) | collective-permute-done | bytes 4194336 | tf_op jit(solution)/shard_map/ppermute | solution.py:126
  209.0 2.9 add.148
  214.0 2.0 fusion.57
  217.1 3.0 convolution_bitcast_fusion
  221.2 1.8 fusion.15
  224.2 2.6 copy.56
  227.1 6.5 %multiply_reduce_fusion.8 = (f32[128]{0:T(128)S(1)}, f32[1,128,32,64]{1,3,2,0:T(8,128)}) fusion(f32[1,128,32,64]{1,3,2,0:T(8,128)} %bitcast.132, f32[32]{0:T(128)S(1)} %copy-done.21, f32[128,32,64]{0,2,1:T(8,128)} %bitcast.133, f32[128,32]{0,1:T(8,128)S(1)} %copy.59, f32[128,32]{0,1:T(8,128)S(1)} %copy.54, f32[128,128]{1,0:T(8,128)S(1)} %fusion.45, ...), kind=kOutput, calls=%fused_computation.51 | convolution fusion | flops 405798784 | bytes 3261056 | tf_op jit(solution)/shard_map/vmap(jvp(tsh,shp->thp))/dot_general | solution.py:51
  235.2 69.0 %collective-permute-done.2 = f32[8,128,1024]{2,1,0:T(8,128)} collective-permute-done((f32[8,128,1024]{2,1,0:T(8,128)}, f32[8,128,1024]{2,1,0:T(8,128)}, u32[]{:S(2)}, u32[]{:S(2)}) %collective-permute-start.2) | collective-permute-done | bytes 4194336 | tf_op jit(solution)/shard_map/ppermute | solution.py:126
  304.2 3.3 fusion.36
  310.4 2.6 copy.64
  313.1 6.1 %fusion.12 = (f32[128,32]{0,1:T(8,128)S(1)}, f32[128,32]{0,1:T(8,128)S(1)}, f32[128,32]{0,1:T(8,128)S(1)}, f32[128,128]{1,0:T(8,128)S(1)}) fusion(f32[128,32]{0,1:T(8,128)S(1)} %copy.59, f32[128,32]{0,1:T(8,128)S(1)} %copy.54, f32[128,128]{1,0:T(8,128)S(1)} %fusion.45, pred[128,128]{1,0:T(8,128)(4,1)S(1)} %iota_compare_fusion, ...), kind=kOutput, calls=%fused_computation.26 | convolution fusion | flops 409440256 | bytes 2326528 | tf_op jit(solution)/shard_map/vmap(transpose(jvp(tsh,shp->thp)))/dot_general | solution.py:51
  321.4 3.4 fusion.9
  324.8 2.6 copy.68
  328.8 2.6 multiply_reduce_fusion.4
  334.3 4.5 fusion.58
  338.9 39.8 %all-reduce.16 = (f32[4,2304]{1,0:T(4,128)S(1)}, f32[2048]{0:T(1024)S(1)}) all-reduce(f32[4,2304]{1,0:T(4,128)S(1)} %add_bitcast_fusion, f32[2048]{0:T(1024)S(1)} %get-tuple-element.11), channel_id=3, replica_groups=mesh['series'=4,'head'=8] {'series','head'}, use_global_device_ids=true, to_apply=%region_15.16.clone | all-reduce | flops 11264 | bytes 90112
  380.0 50.7 %reduce-scatter.4.cloned.1.call-done = f32[32,288]{1,0:T(8,128)} async-done(((f32[1024,288]{1,0:T(8,128)}), f32[32,288]{1,0:T(8,128)}) %reduce-scatter.4.cloned.1.call-update) | async-done | bytes 36880 | tf_op jit(solution)/shard_map/reduce_scatter | solution.py:157
  430.7 150.7 %reduce-scatter.6.cloned.1.call-done = f32[64,1024]{1,0:T(8,128)} async-done(((f32[2048,1024]{1,0:T(8,128)}), f32[64,1024]{1,0:T(8,128)}) %reduce-scatter.6.cloned.1.call-update) | async-done | bytes 262160 | tf_op jit(solution)/shard_map/reduce_scatter | solution.py:160
  (97 shorter events, 21.9 us)
Async XLA Ops:
  7.2 78.3 %copy-start = (bf16[1024,1024]{1,0:T(8,128)(2,1)S(1)}, bf16[1024,1024]{1,0:T(8,128)(2,1)}, u32[]{:S(2)}) copy-start(bf16[1024,1024]{1,0:T(8,128)(2,1)} %param.24) | copy-start | bytes 6291460
  7.2 59.8 %all-gather.2.cloned.1.call-start = ((), (), s32[]{:S(2)}) async-start(), calls=%async_computation.2 | async-start | bytes 9437184 | tf_op jit(solution)/shard_map/all_gather | solution.py:118
  7.2 65.0 %copy-start.19 = (f32[4096]{0:T(1024)S(1)}, f32[4096]{0:T(1024)}, u32[]{:S(2)}) copy-start(f32[4096]{0:T(1024)} %param.21) | copy-start | bytes 49156
  7.9 422.8 %reduce-scatter.4.cloned.1.call-start = ((), (), s32[]{:S(2)}) async-start(), calls=%async_computation.3 | async-start | bytes 1622016 | tf_op jit(solution)/shard_map/reduce_scatter | solution.py:157
  67.0 5.8 copy-start.3
  85.5 18.4 %copy-start.11 = (bf16[512,1024]{1,0:T(8,128)(2,1)S(1)}, bf16[512,1024]{1,0:T(8,128)(2,1)}, u32[]{:S(2)}) copy-start(bf16[512,1024]{1,0:T(8,128)(2,1)} %param.25) | copy-start | bytes 3145732
  107.6 7.2 %collective-permute-start = (f32[8,128,1024]{2,1,0:T(8,128)S(1)}, f32[8,128,1024]{2,1,0:T(8,128)S(1)}, u32[]{:S(2)}, u32[]{:S(2)}) collective-permute-start(f32[8,128,1024]{2,1,0:T(8,128)S(1)} %bitcast.125), channel_id=1, source_target_pairs={{0,1},{1,0},{2,3},{3,2},{4,5},{5,4},{6,7},{7,6},{8,9},{9,8},{10,11... | collective-permute-start | bytes 12582920 | tf_op jit(solution)/shard_map/ppermute | solution.py:126
  116.2 97.5 %copy-start.12 = (bf16[128,1024]{1,0:T(8,128)(2,1)S(1)}, bf16[128,1024]{1,0:T(8,128)(2,1)}, u32[]{:S(2)}) copy-start(bf16[128,1024]{1,0:T(8,128)(2,1)} %param.30) | copy-start | bytes 786436
  116.2 97.5 %copy-start.13 = (bf16[1024,128]{1,0:T(8,128)(2,1)S(1)}, bf16[1024,128]{1,0:T(8,128)(2,1)}, u32[]{:S(2)}) copy-start(bf16[1024,128]{1,0:T(8,128)(2,1)} %param.29) | copy-start | bytes 786436
  116.2 92.8 %collective-permute-start.1 = (f32[8,128,1024]{2,1,0:T(8,128)S(1)}, f32[8,128,1024]{2,1,0:T(8,128)S(1)}, u32[]{:S(2)}, u32[]{:S(2)}) collective-permute-start(f32[8,128,1024]{2,1,0:T(8,128)S(1)} %add.147), channel_id=1, source_target_pairs={{0,2},{1,3},{2,0},{3,1},{4,6},{5,7},{6,4},{7,5},{8,10},{9,11},{10,... | collective-permute-start | bytes 12582920 | tf_op jit(solution)/shard_map/ppermute | solution.py:126
  211.9 4.1 copy-start.8
  211.9 4.3 copy-start.16
  211.9 4.3 copy-start.18
  211.9 92.3 %collective-permute-start.2 = (f32[8,128,1024]{2,1,0:T(8,128)}, f32[8,128,1024]{2,1,0:T(8,128)}, u32[]{:S(2)}, u32[]{:S(2)}) collective-permute-start(f32[8,128,1024]{2,1,0:T(8,128)} %add.148), channel_id=1, source_target_pairs={{0,4},{1,5},{2,6},{3,7},{4,0},{5,1},{6,2},{7,3},{8,12},{9,13},{10,... | collective-permute-start | bytes 12582920 | tf_op jit(solution)/shard_map/ppermute | solution.py:126
  213.7 2.9 copy-start.17
  214.0 3.0 copy-start.15
  223.0 3.8 copy-start.6
  223.0 4.1 copy-start.21
  233.6 70.6 %copy-start.14 = (f32[2048]{0:T(1024)S(1)}, f32[2048]{0:T(1024)}, u32[]{:S(2)}) copy-start(f32[2048]{0:T(1024)} %param.38) | copy-start | bytes 24580
  235.2 72.3 %copy-start.2 = (bf16[2048,1024]{1,0:T(8,128)(2,1)S(1)}, bf16[2048,1024]{1,0:T(8,128)(2,1)}, u32[]{:S(2)}) copy-start(bf16[2048,1024]{1,0:T(8,128)(2,1)} %param.39) | copy-start | bytes 12582916
  313.1 8.3 %copy-start.10 = (f32[128,2048]{0,1:T(8,128)S(1)}, f32[128,2048]{0,1:T(8,128)}, u32[]{:S(2)}) copy-start(f32[128,2048]{0,1:T(8,128)} %copy.64) | copy-start | bytes 3145732
  324.8 3.9 copy-start.5
  333.6 247.8 %reduce-scatter.6.cloned.1.call-start = ((), (), s32[]{:S(2)}) async-start(), calls=%async_computation.4 | async-start | bytes 8650752 | tf_op jit(solution)/shard_map/reduce_scatter | solution.py:160
  338.8 242.6 %copy-start.1 = (bf16[1024,1024]{1,0:T(8,128)(2,1)S(1)}, bf16[1024,1024]{1,0:T(8,128)(2,1)}, u32[]{:S(2)}) copy-start(bf16[1024,1024]{1,0:T(8,128)(2,1)} %param.24) | copy-start | bytes 6291460
  (4 other events, 8.6 us)
Sparse Core Ops, SparseCore 0:
  9.9 57.0 all-gather.1
  333.7 96.9 reduce-scatter.3
  433.6 147.7 reduce-scatter.5
